TPU v7x, 128 devices: a whole 4x4x4 slice. The times are simulated.
128 devices in a mesh: dp: 16 (over z, x), expert: 8 (over y, core).
Axes of the slice: x: 4, y: 4, z: 4, core: 2. Of those that a mesh axis runs over, the one named last changes fastest.
Arguments:
- tokens: bfloat16 [16384, 1280], P(('dp', 'expert')), may hold values from -6 to 6
- routes: int32 [16384, 2], P(('dp', 'expert')), may hold values from 0 to 31, all different within a row; in each aligned block of 128 rows (0 to 127, 128 to 255, ...) at most 10 rows name the same one
- combine: float32 [16384, 2], P(('dp', 'expert')), may hold values from 0.1 to 1
- w_in: bfloat16 [1280, 163840], P(None, ('dp', 'expert')), may hold values from -0.15625 to 0.15625
- w_out: bfloat16 [163840, 1280], P(('dp', 'expert')), may hold values from -0.078125 to 0.078125
- out_grad: bfloat16 [16384, 1280], P(('dp', 'expert')), may hold values from -6 to 6
- head_w: bfloat16 [1280, 17408], P(None, 'expert'), may hold values from -0.5 to 0.5
- labels: int32 [64, 4], P('dp'), may hold values from 0 to 17407
Outputs:
- mixed_out: bfloat16 [16384, 1280], P(('dp', 'expert'))
- d_tokens: bfloat16 [16384, 1280], P(('dp', 'expert'))
- d_combine: float32 [16384, 2], P(('dp', 'expert'))
- d_w_in: bfloat16 [1280, 163840], P(None, ('dp', 'expert'))
- d_w_out: bfloat16 [163840, 1280], P(('dp', 'expert'))
- image_loss: float32 [64], P('dp')
- d_pooled: float32 [64, 1280], P('dp')
- d_head: bfloat16 [1280, 17408], P('dp', 'expert')
Inputs may be any that keep to these rules, and one draw needn't show every extreme that they name: `routes`: in the 128 rows of each device no expert is named by more than 10 rows, a bound that some block reaches; the two entries of a row differ. `labels`: entries of one image may repeat.
All inputs are finite; a program needn't handle non-finite values.
Results may differ from a plain program's by a relative error of at most 0.015.
Values may be sent and summed in bfloat16 or wider, within the bound.
No kernel may reach another device: no remote copies, remote signals or barrier semaphores. Data moves between devices by JAX's collectives and lax.ppermute only.
A program may use at most 192 MiB of HBM per device.

v0:
```python
import jax
import jax.numpy as jnp
from jax import lax
from jax.sharding import PartitionSpec as P

D = 1280
EXPERTS = 32
PATCHES = 256
CLASSES = 17408
beta_rate = 0.99
norm_eps = 1e-06


def gelu_fn(values):
    return jax.nn.gelu(values, approximate=True)


def normalize(pooled):
    center = jnp.mean(pooled, axis=1, keepdims=True)
    spread = jnp.mean(jnp.square(pooled - center), axis=1, keepdims=True)
    return (pooled - center) * lax.rsqrt(spread + norm_eps)


def weighted_focal(logit_vals, targets, class_weight):
    nll_vals = targets * jax.nn.softplus(-logit_vals) + (1.0 - targets) * jax.nn.softplus(
        logit_vals
    )
    return class_weight[None, :] * jnp.square(1.0 - jnp.exp(-nll_vals)) * nll_vals


def expert_pass(xs_rows, grad_rows, w_first, w_second):
    h_pre = jnp.dot(xs_rows, w_first, preferred_element_type=jnp.float32)
    hidden, gelu_back = jax.vjp(gelu_fn, h_pre)
    hidden_bf = hidden.astype(jnp.bfloat16)
    expert_out = jnp.dot(hidden_bf, w_second, preferred_element_type=jnp.float32)
    d_hidden = lax.dot_general(
        grad_rows, w_second, (((1,), (1,)), ((), ())), preferred_element_type=jnp.float32
    )
    d_pre = gelu_back(d_hidden)[0].astype(jnp.bfloat16)
    d_second = lax.dot_general(
        hidden_bf, grad_rows, (((0,), (0,)), ((), ())), preferred_element_type=jnp.float32
    ).astype(jnp.bfloat16)
    d_first = lax.dot_general(
        xs_rows, d_pre, (((0,), (0,)), ((), ())), preferred_element_type=jnp.float32
    ).astype(jnp.bfloat16)
    d_rows = lax.dot_general(
        d_pre, w_first, (((1,), (1,)), ((), ())), preferred_element_type=jnp.float32
    )
    return (expert_out, d_rows, d_first, d_second)


def to_experts(stacked):
    return lax.all_to_all(stacked, ("dp", "expert"), split_axis=1, concat_axis=1, tiled=True)


def to_sources(partials):
    return lax.all_to_all(partials, ("dp", "expert"), split_axis=0, concat_axis=0, tiled=True)


def shards(tokens, routes, combine, w_in, w_out, out_grad, head_w, labels):
    dp_size = lax.axis_size("dp")
    ex_size = lax.axis_size("expert")
    n_devices = dp_size * ex_size
    tok_rows = tokens.shape[0]
    capacity = 5 * tok_rows // 64
    share_count = n_devices // EXPERTS
    buffer_rows = EXPERTS * capacity
    flat_routes = routes.reshape(tok_rows * 2)
    route_hits = (flat_routes[:, None] == jnp.arange(EXPERTS, dtype=jnp.int32)[None, :]).astype(
        jnp.int32
    )
    earlier = jnp.cumsum(route_hits, axis=0) - route_hits
    slot_pos = jnp.sum(earlier * route_hits, axis=1)
    slot_index = flat_routes * capacity + slot_pos
    pair_table = (jnp.arange(buffer_rows, dtype=jnp.int32)[:, None] == slot_index[None, :]).astype(
        jnp.bfloat16
    )
    token_table = jnp.sum(pair_table.reshape(buffer_rows, tok_rows, 2), axis=2)
    pair_grad = (
        (combine[:, :, None] * out_grad.astype(jnp.float32)[:, None, :])
        .astype(jnp.bfloat16)
        .reshape(tok_rows * 2, D)
    )
    x_buf = jnp.dot(token_table, tokens, preferred_element_type=jnp.float32).astype(jnp.bfloat16)
    g_buf = jnp.dot(pair_table, pair_grad, preferred_element_type=jnp.float32).astype(jnp.bfloat16)
    stacked = jnp.stack([x_buf, g_buf]).reshape(2, EXPERTS, 1, capacity, D)
    stacked = jnp.broadcast_to(stacked, (2, EXPERTS, share_count, capacity, D)).reshape(
        2, n_devices, capacity, D
    )
    arrived = to_experts(stacked)
    xs_rows = arrived[0].reshape(n_devices * capacity, D)
    grad_rows = arrived[1].reshape(n_devices * capacity, D)
    expert_out, d_rows, d_w_in, d_w_out = expert_pass(xs_rows, grad_rows, w_in, w_out)
    back_out = to_sources(expert_out.reshape(n_devices, capacity, D))
    expert_sum = jnp.sum(back_out.reshape(EXPERTS, share_count, capacity, D), axis=1).reshape(
        buffer_rows, D
    )
    expert_vals = jnp.take(expert_sum, slot_index, axis=0).reshape(tok_rows, 2, D)
    mixed_out = (
        tokens.astype(jnp.float32) + jnp.sum(combine[:, :, None] * expert_vals, axis=1)
    ).astype(jnp.bfloat16)
    d_combine = jnp.sum(out_grad.astype(jnp.float32)[:, None, :] * expert_vals, axis=2)
    ex_index = lax.axis_index("expert")
    row_images = ex_size * tok_rows // PATCHES
    token_image = (ex_index * tok_rows + jnp.arange(tok_rows, dtype=jnp.int32)) // PATCHES
    image_table = (jnp.arange(row_images, dtype=jnp.int32)[:, None] == token_image[None, :]).astype(
        jnp.float32
    )
    pooled_part = jnp.dot(
        image_table, mixed_out.astype(jnp.float32), precision=lax.Precision.HIGHEST
    )
    class_cols = head_w.shape[1]
    class_ids = ex_index * class_cols + jnp.arange(class_cols, dtype=jnp.int32)
    targets = jnp.any(labels[:, :, None] == class_ids[None, None, :], axis=1).astype(jnp.float32)
    counts = lax.psum(jnp.sum(targets, axis=0), "dp")
    effective = (1.0 - beta_rate) / (1.0 - jnp.power(beta_rate, counts + 1.0))
    pooled_sum, effective_total = lax.psum((pooled_part, jnp.sum(effective)), "expert")
    back_parts = to_sources(d_rows.reshape(n_devices, capacity, D))
    back_sum = jnp.sum(back_parts.reshape(EXPERTS, share_count, capacity, D), axis=1).reshape(
        buffer_rows, D
    )
    expert_back = jnp.take(back_sum, slot_index, axis=0).reshape(tok_rows, 2, D)
    d_tokens = (out_grad.astype(jnp.float32) + jnp.sum(expert_back, axis=1)).astype(jnp.bfloat16)
    class_weight = effective * CLASSES / effective_total
    pooled = pooled_sum / PATCHES
    normed, norm_back = jax.vjp(normalize, pooled)
    normed_bf = normed.astype(jnp.bfloat16)
    logits = jnp.dot(normed_bf, head_w, preferred_element_type=jnp.float32)
    focal_terms, focal_back = jax.vjp(
        lambda logit_vals: weighted_focal(logit_vals, targets, class_weight), logits
    )
    d_logits = focal_back(jnp.ones_like(focal_terms))[0].astype(jnp.bfloat16)
    normed_part = lax.dot_general(
        d_logits, head_w, (((1,), (1,)), ((), ())), preferred_element_type=jnp.float32
    )
    d_normed, image_loss = lax.psum((normed_part, jnp.sum(focal_terms, axis=1)), "expert")
    d_pooled = norm_back(d_normed)[0]
    d_head = lax.psum_scatter(
        lax.dot_general(
            normed_bf, d_logits, (((0,), (0,)), ((), ())), preferred_element_type=jnp.float32
        ).astype(jnp.bfloat16),
        "dp",
        scatter_dimension=0,
        tiled=True,
    )
    return (mixed_out, d_tokens, d_combine, d_w_in, d_w_out, image_loss, d_pooled, d_head)


def solution(mesh):
    in_specs = (
        P(("dp", "expert"), None),
        P(("dp", "expert"), None),
        P(("dp", "expert"), None),
        P(None, ("dp", "expert")),
        P(("dp", "expert"), None),
        P(("dp", "expert"), None),
        P(None, "expert"),
        P("dp", None),
    )
    out_specs = (
        P(("dp", "expert"), None),
        P(("dp", "expert"), None),
        P(("dp", "expert"), None),
        P(None, ("dp", "expert")),
        P(("dp", "expert"), None),
        P("dp"),
        P("dp", None),
        P("dp", "expert"),
    )
    return jax.shard_map(shards, mesh=mesh, in_specs=in_specs, out_specs=out_specs, check_vma=False)
```

profile of v0, /device:TPU:0, one launch (start us, length us, event | category | flops | bytes accessed | tf_op | source)
XLA Modules:
  0.0 685.1 jit_solution(5458899573106623758)
XLA Ops:
  15.7 2.4 mul.203
  18.0 3.0 mul.204
  21.1 2.7 convolution_convert_fusion.3
  29.6 3.8 broadcast_in_dim.16
  33.5 89.6 %all_to_all.15 = bf16[2,128,10,1280]{3,0,2,1:T(2,128)(2,1)S(1)} all-to-all(bf16[2,128,10,1280]{3,0,2,1:T(2,128)(2,1)S(1)} %bitcast.42), channel_id=1, replica_groups=mesh['dp'=16,'expert'=8] {'dp','expert'}, dimensions={1} | all-to-all | bytes 13107200 | tf_op jit(solution)/shard_map/all_to_all | solution.py:53
  123.1 40.3 %slice_reduce_fusion = (bf16[128,10,1280]{2,1,0:T(8,128)(2,1)}, bf16[128,10,1280]{2,1,0:T(8,128)(2,1)}) fusion(bf16[2,128,10,1280]{3,0,2,1:T(2,128)(2,1)S(1)} %all_to_all.15), kind=kLoop, calls=%fused_computation.16 | loop fusion | bytes 13107200 | tf_op jit(solution)/shard_map/slice | solution.py:92
  163.4 7.0 %reshape_squeeze.7 = bf16[1280,1280]{1,0:T(8,128)(2,1)} reshape(bf16[128,10,1280]{2,1,0:T(8,128)(2,1)} %get-tuple-element.49) | data formatting | bytes 6553600 | tf_op jit(solution)/shard_map/reshape;squeeze | solution.py:92
  170.4 7.0 %reshape_squeeze.6 = bf16[1280,1280]{1,0:T(8,128)(2,1)} reshape(bf16[128,10,1280]{2,1,0:T(8,128)(2,1)} %get-tuple-element.50) | data formatting | bytes 6553600 | tf_op jit(solution)/shard_map/reshape;squeeze | solution.py:91
  177.4 7.6 %fusion.37 = f32[1280,1280]{1,0:T(8,128)S(1)} fusion(bf16[1280,1280]{1,0:T(8,128)(2,1)} %reshape_squeeze.7, bf16[1280,1280]{1,0:T(8,128)(2,1)} %param.15), kind=kOutput, calls=%fused_computation.102 | convolution fusion | flops 4194304000 | bytes 13107200 | tf_op jit(solution)/shard_map/dot_general | solution.py:36
  185.0 9.4 %fusion.6 = (bf16[1280,1280]{1,0:T(8,128)(2,1)S(1)}, f32[1280,1280]{1,0:T(8,128)}) fusion(f32[1280,1280]{1,0:T(8,128)S(1)} %fusion.37, bf16[1280,1280]{1,0:T(8,128)(2,1)S(1)} %copy-done.4, bf16[1280,1280]{1,0:T(8,128)(2,1)S(1)} %copy-done), kind=kOutput, calls=%fused_computation.15 | convolution fusion | flops 4227072000 | bytes 22937600 | tf_op jit(solution)/shard_map/dot_general | solution.py:32
  196.2 6.5 fusion.38
  202.8 8.6 %reshape.154 = f32[128,10,1280]{2,1,0:T(8,128)} reshape(f32[1280,1280]{1,0:T(8,128)} %fusion.38) | data formatting | bytes 13107200 | tf_op jit(solution)/shard_map/reshape | solution.py:118
  211.4 6.3 all-to-all-start.2
  217.7 11.2 %fusion.36 = f32[1280,1280]{1,0:T(8,128)} fusion(bf16[1280,1280]{1,0:T(8,128)(2,1)S(1)} %copy-done.9, f32[1280,1280]{1,0:T(8,128)} %get-tuple-element.63), kind=kOutput, calls=%fused_computation.101 | convolution fusion | flops 4209049600 | bytes 16384000 | tf_op jit(solution)/shard_map/dot_general | solution.py:35
  228.9 8.6 %reshape.150 = f32[128,10,1280]{2,1,0:T(8,128)} reshape(f32[1280,1280]{1,0:T(8,128)} %fusion.36) | data formatting | bytes 13107200 | tf_op jit(solution)/shard_map/reshape | solution.py:94
  237.5 103.3 %all-to-all-done.2 = f32[128,10,1280]{2,1,0:T(8,128)} async-done(((f32[128,10,1280]{2,1,0:T(8,128)}), f32[128,10,1280]{2,1,0:T(8,128)}, u32[]{:S(2)}, u32[]{:S(2)}) %all-to-all-start.2) | async-done | bytes 6553632 | tf_op jit(solution)/shard_map/all_to_all | solution.py:57
  340.8 10.3 %all-to-all-start.1 = ((f32[128,10,1280]{2,1,0:T(8,128)}), f32[128,10,1280]{2,1,0:T(8,128)}, u32[]{:S(2)}, u32[]{:S(2)}) async-start(f32[128,10,1280]{2,1,0:T(8,128)} %reshape.150), calls=%async_computation.1 | async-start | bytes 20971520 | tf_op jit(solution)/shard_map/all_to_all | solution.py:57
  351.4 183.0 %psum.35 = f32[2176]{0:T(1024)S(1)} all-reduce(f32[2176]{0:T(1024)S(1)} %convert_reduce_fusion), channel_id=1, replica_groups=mesh['dp'=16,'expert'=8] {'dp'}, use_global_device_ids=true, to_apply=%region_11.13 | all-reduce | flops 2176 | bytes 17408 | tf_op jit(solution)/shard_map/psum | solution.py:115
  535.0 6.8 bitcast_reduce_fusion
  543.7 6.8 bitcast_reduce_fusion.1
  552.4 2.2 gather_fusion.1
  554.6 2.3 gather_fusion
  556.9 3.1 multiply_reduce_fusion
  562.6 27.7 %all-reduce.2 = (f32[4,1280]{1,0:T(4,128)S(1)}, f32[]{:T(128)}) all-reduce(f32[4,1280]{1,0:T(4,128)S(1)} %fusion.29, f32[]{:T(128)} %fusion.28), channel_id=1, replica_groups=mesh['dp'=16,'expert'=8] {'expert'}, use_global_device_ids=true, to_apply=%region_14.16 | all-reduce | flops 5121 | bytes 40968 | tf_op jit(solution)/shard_map/psum | solution.py:117
  591.3 3.6 multiply_reduce_fusion.2
  595.0 4.1 convolution_convert_fusion
  601.0 8.2 %convolution_convert_fusion.2 = bf16[1280,1280]{1,0:T(8,128)(2,1)} fusion(bf16[1280,1280]{1,0:T(8,128)(2,1)S(1)} %copy-done.5, bf16[1280,1280]{1,0:T(8,128)(2,1)} %copy-done.10), kind=kOutput, calls=%fused_computation.8 | convolution fusion | flops 4195942400 | bytes 9830400 | tf_op jit(solution)/shard_map/dot_general | solution.py:43
  609.2 10.1 %convolution_convert_fusion.1 = bf16[1280,1280]{1,0:T(8,128)(2,1)} fusion(bf16[1280,1280]{1,0:T(8,128)(2,1)S(1)} %copy-done.3, f32[1280,1280]{1,0:T(8,128)} %get-tuple-element.63), kind=kOutput, calls=%fused_computation.7 | convolution fusion | flops 4210688000 | bytes 13107200 | tf_op jit(solution)/shard_map/dot_general | solution.py:40
  620.9 25.1 %all-reduce.1 = (f32[4]{0:T(128)}, f32[4,1280]{1,0:T(4,128)S(1)}) all-reduce(f32[4]{0:T(128)S(1)} %get-tuple-element.64, f32[4,1280]{1,0:T(4,128)S(1)} %fusion.34), channel_id=1, replica_groups=mesh['dp'=16,'expert'=8] {'expert'}, use_global_device_ids=true, to_apply=%region_18.21 | all-reduce | flops 5124 | bytes 40992 | tf_op jit(solution)/shard_map/psum | solution.py:136
  646.8 3.0 reshape.157
  649.8 3.7 reduce_sum.156
  656.6 21.2 %reduce-scatter.4.cloned.1.call-done = bf16[80,2176]{1,0:T(8,128)(2,1)} async-done(((bf16[1280,2176]{1,0:T(8,128)(2,1)}), bf16[80,2176]{1,0:T(8,128)(2,1)}) %reduce-scatter.4.cloned.1.call-update) | async-done | bytes 348176
  (78 shorter events, 31.7 us)
Async XLA Ops:
  7.2 177.8 %copy-start = (bf16[1280,1280]{1,0:T(8,128)(2,1)S(1)}, bf16[1280,1280]{1,0:T(8,128)(2,1)}, u32[]{:S(2)}) copy-start(bf16[1280,1280]{1,0:T(8,128)(2,1)} %param.14) | copy-start | bytes 9830404
  177.4 7.6 %copy-start.4 = (bf16[1280,1280]{1,0:T(8,128)(2,1)S(1)}, bf16[1280,1280]{1,0:T(8,128)(2,1)}, u32[]{:S(2)}) copy-start(bf16[1280,1280]{1,0:T(8,128)(2,1)} %reshape_squeeze.6) | copy-start | bytes 9830404
  194.4 1.8 copy-start.10
  211.4 6.3 copy-start.9
  211.4 129.4 %all-to-all-start.2 = ((f32[128,10,1280]{2,1,0:T(8,128)}), f32[128,10,1280]{2,1,0:T(8,128)}, u32[]{:S(2)}, u32[]{:S(2)}) async-start(f32[128,10,1280]{2,1,0:T(8,128)} %reshape.154), calls=%async_computation.2 | async-start | bytes 20971520 | tf_op jit(solution)/shard_map/all_to_all | solution.py:57
  237.5 113.6 %copy-start.8 = (s32[4,4]{1,0:T(4,128)S(1)}, s32[4,4]{1,0:T(4,128)}, u32[]{:S(2)}) copy-start(s32[4,4]{1,0:T(4,128)} %param.18) | copy-start | bytes 196
  340.8 202.9 %all-to-all-start.1 = ((f32[128,10,1280]{2,1,0:T(8,128)}), f32[128,10,1280]{2,1,0:T(8,128)}, u32[]{:S(2)}, u32[]{:S(2)}) async-start(f32[128,10,1280]{2,1,0:T(8,128)} %reshape.150), calls=%async_computation.1 | async-start | bytes 20971520 | tf_op jit(solution)/shard_map/all_to_all | solution.py:57
  351.1 326.7 %reduce-scatter.4.cloned.1.call-start = ((), (), s32[]{:S(2)}) async-start(), calls=%async_computation.4 | async-start | bytes 5918720
  554.6 2.3 copy-start.2
  556.9 5.5 copy-start.7
  562.5 32.5 %copy-start.6 = (bf16[128,1280]{1,0:T(8,128)(2,1)}, bf16[128,1280]{1,0:T(8,128)(2,1)S(1)}, u32[]{:S(2)}) copy-start(bf16[128,1280]{1,0:T(8,128)(2,1)S(1)} %add_convert_fusion.1) | copy-start | bytes 983044
  599.1 1.9 copy-start.5
  601.0 8.2 %copy-start.3 = (bf16[1280,1280]{1,0:T(8,128)(2,1)S(1)}, bf16[1280,1280]{1,0:T(8,128)(2,1)}, u32[]{:S(2)}) copy-start(bf16[1280,1280]{1,0:T(8,128)(2,1)} %reshape_squeeze.7) | copy-start | bytes 9830404
  601.0 18.3 %slice-start = ((s8[5570560]{0:T(1024)(128)(4,1)}), s8[4194304]{0:T(1024)(128)(4,1)S(1)}, s32[]{:S(2)}) async-start(s8[5570560]{0:T(1024)(128)(4,1)} %bitcast.43), calls=%async_computation.5 | async-start | bytes 8388608
  609.2 10.1 %slice-start.1 = ((s8[5570560]{0:T(1024)(128)(4,1)}), s8[1376256]{0:T(1024)(128)(4,1)S(1)}, s32[]{:S(2)}) async-start(s8[5570560]{0:T(1024)(128)(4,1)} %bitcast.43), calls=%async_computation.6 | async-start | bytes 2752512
  609.2 68.5 %copy-start.1 = (bf16[1280,1280]{1,0:T(8,128)(2,1)S(1)}, bf16[1280,1280]{1,0:T(8,128)(2,1)}, u32[]{:S(2)}) copy-start(bf16[1280,1280]{1,0:T(8,128)(2,1)} %param.14) | copy-start | bytes 9830404
Sparse Core Ops, SparseCore 0:
  599.2 78.4 reduce-scatter.3
where the time goes:
time: 692 us; the launch traced here: 685 us
  blocking collectives  325 us (47%)
  waiting for transfers between devices  124 us (18%)
  local copies, waits for them, and re-layouts  106 us (15%)
  matrix products  67.4 us (10%)
  other arithmetic  30.6 us (4%)
  starting transfers between devices  16.6 us (2%)
  between operations  14.8 us (2%)
    psum x1, blocking collectives, shards(): counts = lax.psum(jnp.sum(targets, axis=0), 'dp')  183 us
    all_to_all x2, waiting for transfers between devices, to_sources(): lax.all_to_all(partials, ('dp', 'expert'), split_axis=0, concat_axis=0, t...  103 us
    all_to_all x1, blocking collectives, to_experts(): lax.all_to_all(stacked, ('dp', 'expert'), split_axis=1, concat_axis=1, ti...  89.6 us
    slice x1, local copies, waits for them, and re-layouts, shards(): grad_rows = arrived[1].reshape(n_devices * capacity, D)  40.3 us
    psum x1, blocking collectives, shards(): lax.psum((pooled_part, jnp.sum(effective)), 'expert')  27.7 us
    psum x1, blocking collectives, shards(): lax.psum((normed_part, jnp.sum(focal_terms, axis=1)), 'expert')  25.1 us
    unnamed x2, waiting for transfers between devices  21.2 us
    all_to_all x2, starting transfers between devices, to_sources(): lax.all_to_all(partials, ('dp', 'expert'), split_axis=0, concat_axis=0, t...  16.5 us
  transfers between devices with their start and end apart: 3, of which 2 were waited for; matrix products, arithmetic and copies ran while one was open for 9% of the time, Pallas kernels for 0%

commit v1 on v0

--- a/solution.py
+++ b/solution.py
@@ -1,3 +1,4 @@
+import functools
 import jax
 import jax.numpy as jnp
 from jax import lax
@@ -9,6 +10,13 @@
 CLASSES = 17408
 beta_rate = 0.99
 norm_eps = 1e-06
+
+
+def _settle_goods(tile_in, device_axis):
+    return jnp.sum(jax.lax.all_gather(tile_in, device_axis), axis=0)
+
+
+name_cube = functools.partial(_settle_goods, device_axis="dp")
 
 
 def gelu_fn(values):
@@ -112,7 +120,7 @@
     class_cols = head_w.shape[1]
     class_ids = ex_index * class_cols + jnp.arange(class_cols, dtype=jnp.int32)
     targets = jnp.any(labels[:, :, None] == class_ids[None, None, :], axis=1).astype(jnp.float32)
-    counts = lax.psum(jnp.sum(targets, axis=0), "dp")
+    counts = name_cube(jnp.sum(targets, axis=0))
     effective = (1.0 - beta_rate) / (1.0 - jnp.power(beta_rate, counts + 1.0))
     pooled_sum, effective_total = lax.psum((pooled_part, jnp.sum(effective)), "expert")
     back_parts = to_sources(d_rows.reshape(n_devices, capacity, D))

time: 692 us -> 649 us (0.938)
  blocking collectives: 325 us -> 279 us
    psum x1 -> x0, blocking collectives: 183 us -> none  [shards(): counts = lax.psum(jnp.sum(targets, axis=0), 'dp')]
    all_gather x0 -> x1, blocking collectives: none -> 136 us  [_settle_goods(): return jnp.sum(jax.lax.all_gather(tile_in, device_axis), axis=0)]
where the time goes in v1:
time: 649 us; the launch traced here: 643 us
  blocking collectives  279 us (43%)
  waiting for transfers between devices  129 us (20%)
  local copies, waits for them, and re-layouts  106 us (16%)
  matrix products  67.1 us (10%)
  other arithmetic  30.7 us (5%)
  starting transfers between devices  16.6 us (3%)
  between operations  14.8 us (2%)
    all_gather x1, blocking collectives, _settle_goods(): return jnp.sum(jax.lax.all_gather(tile_in, device_axis), axis=0)  136 us
    all_to_all x2, waiting for transfers between devices, to_sources(): lax.all_to_all(partials, ('dp', 'expert'), split_axis=0, concat_axis=0, t...  103 us
    all_to_all x1, blocking collectives, to_experts(): lax.all_to_all(stacked, ('dp', 'expert'), split_axis=1, concat_axis=1, ti...  89.6 us
    slice x1, local copies, waits for them, and re-layouts, shards(): grad_rows = arrived[1].reshape(n_devices * capacity, D)  40.3 us
    psum x1, blocking collectives, shards(): lax.psum((pooled_part, jnp.sum(effective)), 'expert')  27.7 us
    unnamed x2, waiting for transfers between devices  25.7 us
    psum x1, blocking collectives, shards(): lax.psum((normed_part, jnp.sum(focal_terms, axis=1)), 'expert')  25.2 us
    all_to_all x2, starting transfers between devices, to_sources(): lax.all_to_all(partials, ('dp', 'expert'), split_axis=0, concat_axis=0, t...  16.5 us
  transfers between devices with their start and end apart: 3, of which 2 were waited for; matrix products, arithmetic and copies ran while one was open for 9% of the time, Pallas kernels for 0%

profile of v1, /device:TPU:0, one launch (start us, length us, event | category | flops | bytes accessed | tf_op | source)
XLA Modules:
  0.0 642.6 jit_solution(10079464533597648352)
XLA Ops:
  15.7 2.4 mul.207
  18.0 3.0 mul.208
  21.1 2.7 convolution_convert_fusion.3
  29.6 3.8 broadcast_in_dim.16
  33.5 89.6 %all_to_all.15 = bf16[2,128,10,1280]{3,0,2,1:T(2,128)(2,1)S(1)} all-to-all(bf16[2,128,10,1280]{3,0,2,1:T(2,128)(2,1)S(1)} %bitcast.42), channel_id=1, replica_groups=mesh['dp'=16,'expert'=8] {'dp','expert'}, dimensions={1} | all-to-all | bytes 13107200 | tf_op jit(solution)/shard_map/all_to_all | solution.py:61
  123.1 40.3 %slice_reduce_fusion = (bf16[128,10,1280]{2,1,0:T(8,128)(2,1)}, bf16[128,10,1280]{2,1,0:T(8,128)(2,1)}) fusion(bf16[2,128,10,1280]{3,0,2,1:T(2,128)(2,1)S(1)} %all_to_all.15), kind=kLoop, calls=%fused_computation.16 | loop fusion | bytes 13107200 | tf_op jit(solution)/shard_map/slice | solution.py:100
  163.4 7.0 %reshape_squeeze.7 = bf16[1280,1280]{1,0:T(8,128)(2,1)} reshape(bf16[128,10,1280]{2,1,0:T(8,128)(2,1)} %get-tuple-element.49) | data formatting | bytes 6553600 | tf_op jit(solution)/shard_map/reshape;squeeze | solution.py:100
  170.4 7.0 %reshape_squeeze.6 = bf16[1280,1280]{1,0:T(8,128)(2,1)} reshape(bf16[128,10,1280]{2,1,0:T(8,128)(2,1)} %get-tuple-element.50) | data formatting | bytes 6553600 | tf_op jit(solution)/shard_map/reshape;squeeze | solution.py:99
  177.4 7.6 %fusion.37 = f32[1280,1280]{1,0:T(8,128)S(1)} fusion(bf16[1280,1280]{1,0:T(8,128)(2,1)} %reshape_squeeze.7, bf16[1280,1280]{1,0:T(8,128)(2,1)} %param.15), kind=kOutput, calls=%fused_computation.102 | convolution fusion | flops 4194304000 | bytes 13107200 | tf_op jit(solution)/shard_map/dot_general | solution.py:44
  185.0 9.4 %fusion.6 = (bf16[1280,1280]{1,0:T(8,128)(2,1)S(1)}, f32[1280,1280]{1,0:T(8,128)}) fusion(f32[1280,1280]{1,0:T(8,128)S(1)} %fusion.37, bf16[1280,1280]{1,0:T(8,128)(2,1)S(1)} %copy-done.4, bf16[1280,1280]{1,0:T(8,128)(2,1)S(1)} %copy-done), kind=kOutput, calls=%fused_computation.15 | convolution fusion | flops 4227072000 | bytes 22937600 | tf_op jit(solution)/shard_map/dot_general | solution.py:40
  196.2 6.5 %fusion.38 = f32[1280,1280]{1,0:T(8,128)} fusion(bf16[1280,1280]{1,0:T(8,128)(2,1)S(1)} %get-tuple-element.62, bf16[1280,1280]{1,0:T(8,128)(2,1)S(1)} %copy-done), kind=kOutput, calls=%fused_computation.103 | convolution fusion | flops 4194304000 | bytes 13107200 | tf_op jit(solution)/shard_map/dot_general | solution.py:54
  202.8 8.6 %reshape.161 = f32[128,10,1280]{2,1,0:T(8,128)} reshape(f32[1280,1280]{1,0:T(8,128)} %fusion.38) | data formatting | bytes 13107200 | tf_op jit(solution)/shard_map/reshape | solution.py:126
  211.4 6.3 all-to-all-start.2
  217.7 11.2 %fusion.36 = f32[1280,1280]{1,0:T(8,128)} fusion(bf16[1280,1280]{1,0:T(8,128)(2,1)S(1)} %copy-done.9, f32[1280,1280]{1,0:T(8,128)} %get-tuple-element.63), kind=kOutput, calls=%fused_computation.101 | convolution fusion | flops 4209049600 | bytes 16384000 | tf_op jit(solution)/shard_map/dot_general | solution.py:43
  228.9 8.6 %reshape.157 = f32[128,10,1280]{2,1,0:T(8,128)} reshape(f32[1280,1280]{1,0:T(8,128)} %fusion.36) | data formatting | bytes 13107200 | tf_op jit(solution)/shard_map/reshape | solution.py:102
  237.5 103.3 %all-to-all-done.2 = f32[128,10,1280]{2,1,0:T(8,128)} async-done(((f32[128,10,1280]{2,1,0:T(8,128)}), f32[128,10,1280]{2,1,0:T(8,128)}, u32[]{:S(2)}, u32[]{:S(2)}) %all-to-all-start.2) | async-done | bytes 6553632 | tf_op jit(solution)/shard_map/all_to_all | solution.py:65
  340.8 10.3 %all-to-all-start.1 = ((f32[128,10,1280]{2,1,0:T(8,128)}), f32[128,10,1280]{2,1,0:T(8,128)}, u32[]{:S(2)}, u32[]{:S(2)}) async-start(f32[128,10,1280]{2,1,0:T(8,128)} %reshape.157), calls=%async_computation.1 | async-start | bytes 20971520 | tf_op jit(solution)/shard_map/all_to_all | solution.py:65
  351.4 136.0 %all-gather.1 = f32[16,1,2176]{2,1,0:T(1,128)S(1)} all-gather(f32[1,1,2176]{2,1,0:T(1,128)S(1)} %reshape.184), channel_id=2, replica_groups=mesh['dp'=16,'expert'=8] {'dp'}, dimensions={0}, use_global_device_ids=true | all-gather | bytes 147968 | tf_op jit(solution)/shard_map/all_gather | solution.py:16
  488.1 6.8 %bitcast_reduce_fusion = f32[32,10,1280]{2,1,0:T(8,128)} fusion(f32[128,10,1280]{2,1,0:T(8,128)} %all-to-all-done.2), kind=kLoop, calls=%fused_computation.3 | loop fusion | flops 1228800 | bytes 8192000 | tf_op jit(solution)/shard_map/reduce_sum | solution.py:127
  496.8 6.8 %bitcast_reduce_fusion.1 = f32[32,10,1280]{2,1,0:T(8,128)} fusion(f32[128,10,1280]{2,1,0:T(8,128)} %all-to-all-done.1), kind=kLoop, calls=%fused_computation.4 | loop fusion | flops 1228800 | bytes 8192000 | tf_op jit(solution)/shard_map/reduce_sum | solution.py:103
  505.5 2.2 gather_fusion.1
  507.8 2.3 gather_fusion
  510.0 3.1 multiply_reduce_fusion
  515.8 27.7 %all-reduce.2 = (f32[4,1280]{1,0:T(4,128)S(1)}, f32[]{:T(128)}) all-reduce(f32[4,1280]{1,0:T(4,128)S(1)} %fusion.29, f32[]{:T(128)} %fusion.28), channel_id=1, replica_groups=mesh['dp'=16,'expert'=8] {'expert'}, use_global_device_ids=true, to_apply=%region_14.16 | all-reduce | flops 5121 | bytes 40968 | tf_op jit(solution)/shard_map/psum | solution.py:125
  544.5 3.6 multiply_reduce_fusion.2
  548.1 4.1 convolution_convert_fusion
  554.2 8.0 %convolution_convert_fusion.2 = bf16[1280,1280]{1,0:T(8,128)(2,1)} fusion(bf16[1280,1280]{1,0:T(8,128)(2,1)S(1)} %copy-done.5, bf16[1280,1280]{1,0:T(8,128)(2,1)} %copy-done.10), kind=kOutput, calls=%fused_computation.8 | convolution fusion | flops 4195942400 | bytes 9830400 | tf_op jit(solution)/shard_map/dot_general | solution.py:51
  562.2 10.1 %convolution_convert_fusion.1 = bf16[1280,1280]{1,0:T(8,128)(2,1)} fusion(bf16[1280,1280]{1,0:T(8,128)(2,1)S(1)} %copy-done.3, f32[1280,1280]{1,0:T(8,128)} %get-tuple-element.63), kind=kOutput, calls=%fused_computation.7 | convolution fusion | flops 4210688000 | bytes 13107200 | tf_op jit(solution)/shard_map/dot_general | solution.py:48
  573.9 25.2 %all-reduce.1 = (f32[4]{0:T(128)}, f32[4,1280]{1,0:T(4,128)S(1)}) all-reduce(f32[4]{0:T(128)S(1)} %get-tuple-element.64, f32[4,1280]{1,0:T(4,128)S(1)} %fusion.34), channel_id=1, replica_groups=mesh['dp'=16,'expert'=8] {'expert'}, use_global_device_ids=true, to_apply=%region_18.21 | all-reduce | flops 5124 | bytes 40992 | tf_op jit(solution)/shard_map/psum | solution.py:144
  599.8 3.0 reshape.164
  602.8 3.7 reduce_sum.165
  609.7 25.7 %reduce-scatter.4.cloned.1.call-done = bf16[80,2176]{1,0:T(8,128)(2,1)} async-done(((bf16[1280,2176]{1,0:T(8,128)(2,1)}), bf16[80,2176]{1,0:T(8,128)(2,1)}) %reduce-scatter.4.cloned.1.call-update) | async-done | bytes 348176
  (80 shorter events, 31.8 us)
Async XLA Ops:
  7.2 177.8 %copy-start = (bf16[1280,1280]{1,0:T(8,128)(2,1)S(1)}, bf16[1280,1280]{1,0:T(8,128)(2,1)}, u32[]{:S(2)}) copy-start(bf16[1280,1280]{1,0:T(8,128)(2,1)} %param.14) | copy-start | bytes 9830404
  177.4 7.6 %copy-start.4 = (bf16[1280,1280]{1,0:T(8,128)(2,1)S(1)}, bf16[1280,1280]{1,0:T(8,128)(2,1)}, u32[]{:S(2)}) copy-start(bf16[1280,1280]{1,0:T(8,128)(2,1)} %reshape_squeeze.6) | copy-start | bytes 9830404
  194.4 1.8 copy-start.10
  211.4 6.3 copy-start.9
  211.4 129.4 %all-to-all-start.2 = ((f32[128,10,1280]{2,1,0:T(8,128)}), f32[128,10,1280]{2,1,0:T(8,128)}, u32[]{:S(2)}, u32[]{:S(2)}) async-start(f32[128,10,1280]{2,1,0:T(8,128)} %reshape.161), calls=%async_computation.2 | async-start | bytes 20971520 | tf_op jit(solution)/shard_map/all_to_all | solution.py:65
  237.5 113.6 %copy-start.8 = (s32[4,4]{1,0:T(4,128)S(1)}, s32[4,4]{1,0:T(4,128)}, u32[]{:S(2)}) copy-start(s32[4,4]{1,0:T(4,128)} %param.18) | copy-start | bytes 196
  340.8 156.0 %all-to-all-start.1 = ((f32[128,10,1280]{2,1,0:T(8,128)}), f32[128,10,1280]{2,1,0:T(8,128)}, u32[]{:S(2)}, u32[]{:S(2)}) async-start(f32[128,10,1280]{2,1,0:T(8,128)} %reshape.157), calls=%async_computation.1 | async-start | bytes 20971520 | tf_op jit(solution)/shard_map/all_to_all | solution.py:65
  351.1 284.3 %reduce-scatter.4.cloned.1.call-start = ((), (), s32[]{:S(2)}) async-start(), calls=%async_computation.4 | async-start | bytes 5918720
  507.8 2.3 copy-start.2
  510.0 5.5 copy-start.7
  515.6 32.5 %copy-start.6 = (bf16[128,1280]{1,0:T(8,128)(2,1)}, bf16[128,1280]{1,0:T(8,128)(2,1)S(1)}, u32[]{:S(2)}) copy-start(bf16[128,1280]{1,0:T(8,128)(2,1)S(1)} %add_convert_fusion.1) | copy-start | bytes 983044
  552.3 1.9 copy-start.5
  554.2 8.0 %copy-start.3 = (bf16[1280,1280]{1,0:T(8,128)(2,1)S(1)}, bf16[1280,1280]{1,0:T(8,128)(2,1)}, u32[]{:S(2)}) copy-start(bf16[1280,1280]{1,0:T(8,128)(2,1)} %reshape_squeeze.7) | copy-start | bytes 9830404
  554.2 18.1 %slice-start = ((s8[5570560]{0:T(1024)(128)(4,1)}), s8[4194304]{0:T(1024)(128)(4,1)S(1)}, s32[]{:S(2)}) async-start(s8[5570560]{0:T(1024)(128)(4,1)} %bitcast.43), calls=%async_computation.5 | async-start | bytes 8388608
  562.2 10.1 %slice-start.1 = ((s8[5570560]{0:T(1024)(128)(4,1)}), s8[1376256]{0:T(1024)(128)(4,1)S(1)}, s32[]{:S(2)}) async-start(s8[5570560]{0:T(1024)(128)(4,1)} %bitcast.43), calls=%async_computation.6 | async-start | bytes 2752512
  562.2 73.1 %copy-start.1 = (bf16[1280,1280]{1,0:T(8,128)(2,1)S(1)}, bf16[1280,1280]{1,0:T(8,128)(2,1)}, u32[]{:S(2)}) copy-start(bf16[1280,1280]{1,0:T(8,128)(2,1)} %param.14) | copy-start | bytes 9830404
Sparse Core Ops, SparseCore 0:
  552.4 82.8 reduce-scatter.3
